TPU v7x, 32 devices: a whole 2x2x4 slice. The times are simulated.
32 devices in a mesh: row: 4 (over y, x), col: 8 (over z, core).
Axes of the slice: x: 2, y: 2, z: 4, core: 2. Of those that a mesh axis runs over, the one named last changes fastest.
Arguments:
- trailing_slab: bfloat16 [24576, 8192], P('row', 'col'), may hold values from -6 to 6
- panel_cols: bfloat16 [24576, 512], P('row', 'col'), may hold values from -0.25 to 0.25
- head_slab: bfloat16 [512, 8192], P('row', 'col'), may hold values from -6 to 6
- coupling: bfloat16 [2, 256, 256], replicated, may hold values from -0.25 to 0.25
- lower_inverses: bfloat16 [2, 256, 256], replicated, may hold values from -1.5 to 1.5, as said below
- upper_inverses: bfloat16 [2, 256, 256], replicated, may hold values from -1.5 to 1.5, as said below
Outputs:
- trailing: bfloat16 [24576, 8192], P('row', 'col')
Inputs may be any that keep to these rules, and one draw needn't show every extreme that they name: `lower_inverses`: each of the two [256, 256] blocks is lower triangular with unit diagonal. `upper_inverses`: each of the two [256, 256] blocks is upper triangular with diagonal between 0.5 and 1.5.
All inputs are finite; a program needn't handle non-finite values.
Results may differ from a plain program's by a relative error of at most 0.0067.
Values may be sent and summed in bfloat16 or wider, within the bound.
No kernel may reach another device: no remote copies, remote signals or barrier semaphores. Data moves between devices by JAX's collectives and lax.ppermute only.
A program may use at most 128 MiB of HBM per device.

v0:
```python
import jax
import jax.numpy as jnp
from jax import lax
from jax.sharding import PartitionSpec as P


def product(left, right):
    return jnp.dot(left, right, preferred_element_type=jnp.float32)


def factor_panel(panel_block, upper_mid, upper_inverses):
    width = upper_mid.shape[0]
    lower_first = product(panel_block[:, :width], upper_inverses[0]).astype(jnp.bfloat16)
    panel_second = (
        panel_block[:, width:].astype(jnp.float32) - product(lower_first, upper_mid)
    ).astype(jnp.bfloat16)
    lower_second = product(panel_second, upper_inverses[1]).astype(jnp.bfloat16)
    return jnp.concatenate([lower_first, lower_second], axis=1)


def apply_update(slab_part, lower_block, upper_both):
    result = slab_part.astype(jnp.float32) - product(lower_block, upper_both)
    return result.astype(jnp.bfloat16)


def on_device(trailing_slab, panel_cols, head_slab, coupling, lower_inverses, upper_inverses):
    width = coupling.shape[1]
    head_full = lax.all_gather(head_slab, "row", axis=0, tiled=True)
    upper_mid = product(lower_inverses[0], coupling[0]).astype(jnp.bfloat16)
    upper_first = product(lower_inverses[0], head_full[:width]).astype(jnp.bfloat16)
    lower_head = product(coupling[1], upper_inverses[0]).astype(jnp.bfloat16)
    head_second = (head_full[width:].astype(jnp.float32) - product(lower_head, upper_first)).astype(
        jnp.bfloat16
    )
    upper_second = product(lower_inverses[1], head_second).astype(jnp.bfloat16)
    upper_both = jnp.concatenate([upper_first, upper_second], axis=0)
    panel_full = lax.all_gather(panel_cols, "col", axis=1, tiled=True)
    lower_block = factor_panel(panel_full, upper_mid, upper_inverses)
    return apply_update(trailing_slab, lower_block, upper_both)


def solution(mesh):
    in_specs = (P("row", "col"), P("row", "col"), P("row", "col"), P(), P(), P())
    out_specs = P("row", "col")
    return jax.shard_map(
        on_device, mesh=mesh, in_specs=in_specs, out_specs=out_specs, check_vma=False
    )
```

profile of v0, /device:TPU:0, one launch (start us, length us, event | category | flops | bytes accessed | tf_op | source)
XLA Modules:
  0.0 133.2 jit_solution(17150895435019928692)
XLA Ops:
  6.5 0.0 all-gather.5.cloned.1.call-start
  6.5 0.7 all-gather.5.cloned.1.call-update
  7.3 0.0 all-gather.3.cloned.1.call-start
  7.3 0.7 all-gather.3.cloned.1.call-update
  8.0 1.2 convolution_convert_fusion.4
  9.2 1.2 convolution_convert_fusion.5
  10.3 0.0 copy-start.1
  10.3 28.1 %all-gather.5.cloned.1.call-done = bf16[512,1024]{1,0:T(8,128)(2,1)} async-done(((bf16[128,1024]{1,0:T(8,128)(2,1)}), bf16[512,1024]{1,0:T(8,128)(2,1)}) %all-gather.5.cloned.1.call-update) | async-done | bytes 1048592 | tf_op jit(solution)/shard_map/all_gather | solution.py:28
  38.4 1.4 %convolution_convert_fusion.3 = bf16[256,1024]{1,0:T(8,128)(2,1)S(1)} fusion(bf16[512,1024]{1,0:T(8,128)(2,1)} %all-gather.5.cloned.1.call-done, bf16[2,256,256]{2,1,0:T(8,128)(2,1)} %param.10), kind=kOutput, calls=%fused_computation.11 | convolution fusion | flops 134479872 | bytes 1179648 | tf_op jit(solution)/shard_map/dot_general | solution.py:8
  39.9 0.0 copy-start
  39.9 2.6 %fusion.6 = bf16[256,1024]{1,0:T(8,128)(2,1)} fusion(bf16[256,256]{1,0:T(8,128)(2,1)S(1)} %convolution_convert_fusion.4, bf16[256,1024]{1,0:T(8,128)(2,1)S(1)} %convolution_convert_fusion.3, bf16[512,1024]{1,0:T(8,128)(2,1)} %all-gather.5.cloned.1.call-done, bf16[2,256,256]{2,1,0:T(8,128)(2,1)} %param.10), kind=kOutput, calls=%fused_computation.13 | convolution fusion | flops 269484032 | bytes 1835008 | tf_op jit(solution)/shard_map/dot_general | solution.py:8
  42.5 0.0 copy-done
  42.5 62.3 %all-gather.3.cloned.1.call-done = bf16[6144,512]{0,1:T(8,128)(2,1)} async-done(((bf16[6144,64]{0,1:T(8,128)(2,1)}), bf16[6144,512]{0,1:T(8,128)(2,1)}) %all-gather.3.cloned.1.call-update) | async-done | bytes 6291472 | tf_op jit(solution)/shard_map/all_gather | solution.py:37
  104.8 2.9 %convolution_convert_fusion.1 = bf16[6144,256]{0,1:T(8,128)(2,1)S(1)} fusion(bf16[6144,512]{0,1:T(8,128)(2,1)} %all-gather.3.cloned.1.call-done, bf16[2,256,256]{2,1,0:T(8,128)(2,1)} %param.11), kind=kOutput, calls=%fused_computation.4 | convolution fusion | flops 806879232 | bytes 6422528 | tf_op jit(solution)/shard_map/dot_general | solution.py:8
  107.7 0.0 copy-done.1
  107.7 5.5 %convolution_convert_fusion = bf16[6144,256]{0,1:T(8,128)(2,1)} fusion(bf16[6144,256]{0,1:T(8,128)(2,1)S(1)} %convolution_convert_fusion.1, bf16[256,256]{1,0:T(8,128)(2,1)S(1)} %convolution_convert_fusion.5, bf16[6144,512]{0,1:T(8,128)(2,1)} %all-gather.3.cloned.1.call-done, bf16[2,256,256]{2,1,0:T(8,128)(2,1)S(1)} %copy-done.1), kind=kOutput, calls=%fused_computation.3 | convolution fusion | flops 1616904192 | bytes 9699328 | tf_op jit(solution)/shard_map/dot_general | solution.py:8
  113.2 13.2 %subtract_convert_fusion = bf16[6144,1024]{1,0:T(8,128)(2,1)} fusion(bf16[6144,1024]{1,0:T(8,128)(2,1)} %param.6, bf16[6144,256]{0,1:T(8,128)(2,1)} %convolution_convert_fusion, bf16[6144,256]{0,1:T(8,128)(2,1)S(1)} %convolution_convert_fusion.1, bf16[256,1024]{1,0:T(8,128)(2,1)} %fusion.6, bf16[256,1024]{1,0:T(8,128)(2,1)} %copy-done), kind=kOutput, calls=%fused_computation | convolution fusion | flops 6476005376 | bytes 32505856 | tf_op jit(solution)/shard_map/dot_general | solution.py:8
Async XLA Ops:
  6.5 31.9 %all-gather.5.cloned.1.call-start = ((), (), s32[]{:S(2)}) async-start(), calls=%async_computation.1 | async-start | bytes 1310720 | tf_op jit(solution)/shard_map/all_gather | solution.py:28
  7.3 97.5 %all-gather.3.cloned.1.call-start = ((), (), s32[]{:S(2)}) async-start(), calls=%async_computation | async-start | bytes 7077888 | tf_op jit(solution)/shard_map/all_gather | solution.py:37
  10.3 97.4 %copy-start.1 = (bf16[2,256,256]{2,1,0:T(8,128)(2,1)S(1)}, bf16[2,256,256]{2,1,0:T(8,128)(2,1)}, u32[]{:S(2)}) copy-start(bf16[2,256,256]{2,1,0:T(8,128)(2,1)} %param.11) | copy-start | bytes 786436
  39.9 2.6 %copy-start = (bf16[256,1024]{1,0:T(8,128)(2,1)}, bf16[256,1024]{1,0:T(8,128)(2,1)S(1)}, u32[]{:S(2)}) copy-start(bf16[256,1024]{1,0:T(8,128)(2,1)S(1)} %convolution_convert_fusion.3) | copy-start | bytes 1572868
Sparse Core Ops, SparseCore 0:
  9.2 29.2 all-gather.4
  40.1 64.6 all-gather.2
where the time goes:
time: 133 us
  waiting for transfers between devices  91.8 us (69%)
  matrix products  27.9 us (21%)
  between operations  13.5 us (10%)
    all_gather x1, waiting for transfers between devices, on_device(): panel_full = lax.all_gather(panel_cols, 'col', axis=1, tiled=True)  62.3 us
    all_gather x1, waiting for transfers between devices, on_device(): head_full = lax.all_gather(head_slab, 'row', axis=0, tiled=True)  28.1 us
    dot_general x7, matrix products, product(): return jnp.dot(left, right, preferred_element_type=jnp.float32)  27.9 us
  transfers between devices with their start and end apart: 2, of which 2 were waited for; matrix products, arithmetic and copies ran while one was open for 5% of the time, Pallas kernels for 0%

commit v1 on v0

v1 whole, which is shorter than its diff:
```python
import functools

import jax
import jax.numpy as jnp
from jax import lax
from jax.experimental import pallas as pl
from jax.experimental.pallas import tpu as pltpu
from jax.sharding import PartitionSpec as P


CORES = 2
F32 = jnp.float32
BF16 = jnp.bfloat16


def product(left, right):
    return jnp.dot(left, right, preferred_element_type=F32)


def product_wide(left, right):
    high = right.astype(BF16)
    low = (right - high.astype(F32)).astype(BF16)
    return product(left, high) + product(left, low)


def weights_kernel(parts, chips, ids_ref, *refs):
    row, col = ids_ref[0], ids_ref[1]
    chip, core = lax.div(col, CORES), lax.rem(col, CORES)
    head_refs = refs[:parts]
    coupling_ref, lower_ref, upper_ref, out_ref, head, both = refs[parts:]
    rows = head_refs[0].shape[0]
    width = coupling_ref.shape[1]
    for at in range(parts):
        start = pl.multiple_of((row ^ at) * rows, rows)
        head[pl.ds(start, rows), :] = head_refs[at][...]
    upper_mid = product(lower_ref[0], coupling_ref[0]).astype(BF16)
    lower_head = product(coupling_ref[1], upper_ref[0]).astype(BF16)
    upper_first = product(lower_ref[0], head[:width, :]).astype(BF16)
    head_second = (head[width:, :].astype(F32) - product(lower_head, upper_first)).astype(BF16)
    upper_second = product(lower_ref[1], head_second).astype(BF16)
    second = product(upper_ref[1], upper_second)
    rest = upper_first.astype(F32) - product_wide(upper_mid, second)
    both[:width, :] = product_wide(upper_ref[0], rest).astype(BF16)
    both[width:, :] = second.astype(BF16)
    depth = out_ref.shape[0] // (chips * CORES)
    for at in range(chips * CORES):
        source = lax.rem(chip + chips - at // CORES, chips) * CORES + (core ^ (at % CORES))
        start = pl.multiple_of(source * depth, depth)
        out_ref[at * depth : (at + 1) * depth, :] = both[pl.ds(start, depth), :]


def weights(ids, heads, coupling, lower_inverses, upper_inverses, chips):
    depth = 2 * coupling.shape[1]
    columns = heads[0].shape[1]
    vmem = pl.BlockSpec(memory_space=pltpu.VMEM)
    return pl.pallas_call(
        functools.partial(weights_kernel, len(heads), chips),
        out_shape=jax.ShapeDtypeStruct((depth, columns), BF16),
        in_specs=[pl.BlockSpec(memory_space=pltpu.SMEM)] + [vmem] * (len(heads) + 3),
        out_specs=vmem,
        scratch_shapes=[pltpu.VMEM((depth, columns), BF16), pltpu.VMEM((depth, columns), BF16)],
        compiler_params=pltpu.CompilerParams(vmem_limit_bytes=16 << 20),
        cost_estimate=pl.CostEstimate(flops=2 * 10 * 256 * 256 * columns, bytes_accessed=8 * columns * 256, transcendentals=0),
        name="weights",
    )(ids, *heads, coupling, lower_inverses, upper_inverses)


def update_kernel(pieces, slab_ref, weights_ref, *refs):
    out_ref = refs[-1]
    left = jnp.concatenate([ref[...] for ref in refs[:pieces]], axis=0)
    change = lax.dot_general(left, weights_ref[...], (((0,), (0,)), ((), ())), preferred_element_type=F32)
    out_ref[...] = (slab_ref[...].astype(F32) - change).astype(BF16)


def update(slab, weights_all, pieces, start, rows, result):
    columns = slab.shape[1]
    tile = min(512, rows)
    first = start // tile
    in_specs = [
        pl.BlockSpec((tile, columns), lambda i: (first + i, 0)),
        pl.BlockSpec(weights_all.shape, lambda i: (0, 0), pipeline_mode=pl.Buffered(1)),
    ]
    for array, offset in pieces:
        at = (start - offset) // tile
        in_specs.append(pl.BlockSpec((array.shape[0], tile), functools.partial(lambda at, i: (0, at + i), at)))
    operands = [slab, weights_all] + [array for array, _ in pieces]
    aliases = {}
    if result is not None:
        in_specs.append(pl.BlockSpec(memory_space=pl.ANY))
        aliases = {len(operands): 0}
        operands.append(result)
    return pl.pallas_call(
        functools.partial(update_kernel, len(pieces)),
        grid=(rows // tile,),
        out_shape=jax.ShapeDtypeStruct(slab.shape, slab.dtype),
        in_specs=in_specs,
        out_specs=pl.BlockSpec((tile, columns), lambda i: (first + i, 0)),
        input_output_aliases=aliases,
        compiler_params=pltpu.CompilerParams(dimension_semantics=("arbitrary",), vmem_limit_bytes=16 << 20),
        cost_estimate=pl.CostEstimate(
            flops=2 * rows * columns * weights_all.shape[0],
            bytes_accessed=2 * rows * columns * 2,
            transcendentals=0,
        ),
        name="update",
    )(*operands)


def later(value, done):
    return lax.optimization_barrier((value, done))[0]


def on_device(rows_of, cols_of, groups, trailing_slab, panel_cols, head_slab, coupling, lower_inverses, upper_inverses):
    chips = cols_of // CORES
    ring = [(c, (c + CORES) % cols_of) for c in range(cols_of)]
    sibling = [(c, c ^ 1) for c in range(cols_of)]
    panel = panel_cols.T

    def send(value, pairs, axis="col"):
        return lax.ppermute(value, axis, pairs)

    arrived = []
    panel_sibling = None
    behind = None
    for g, group in enumerate(groups):
        source = panel if behind is None else later(panel, behind)
        held = [source[:, start : start + size] for start, size in group]
        for step in range(1, chips):
            for i in range(len(group)):
                held[i] = send(held[i], ring)
                if panel_sibling is None:
                    first = held[i]
                    panel_sibling = send(later(panel, first), sibling)
                arrived.append((g, i, held[i], send(held[i], sibling)))
            if step == chips - 2:
                behind = held[-1]

    head_slab = later(head_slab, first)
    heads = [head_slab]
    for shift in range(1, rows_of):
        heads.append(send(head_slab, [(r, r ^ shift) for r in range(rows_of)], "row"))
    ids = jnp.stack([lax.axis_index("row"), lax.axis_index("col")]).astype(jnp.int32)
    weights_all = weights(ids, heads, coupling, lower_inverses, upper_inverses, chips)

    result = None
    for g, group in enumerate(groups):
        for i, (start, size) in enumerate(group):
            pieces = [(panel, 0), (panel_sibling, 0)]
            for at, chunk, own, other in arrived:
                if (at, chunk) == (g, i):
                    pieces += [(own, start), (other, start)]
            result = update(trailing_slab, weights_all, pieces, start, size, result)
    return result


def plan(rows):
    unit = rows // 6
    sizes = [[unit, unit, unit], [unit, unit, unit]]
    groups, start = [], 0
    for group in sizes:
        groups.append([])
        for size in group:
            groups[-1].append((start, size))
            start += size
    return groups


def solution(mesh):
    in_specs = (P("row", "col"), P("row", "col"), P("row", "col"), P(), P(), P())
    out_specs = P("row", "col")
    rows_of, cols_of = mesh.shape["row"], mesh.shape["col"]

    def body(*arrays):
        groups = plan(arrays[0].shape[0])
        return on_device(rows_of, cols_of, groups, *arrays)

    return jax.shard_map(body, mesh=mesh, in_specs=in_specs, out_specs=out_specs, check_vma=False)
```

time: 133 us -> 94.2 us (0.71)
  waiting for transfers between devices: 91.8 us -> 35.8 us
  matrix products: 27.9 us -> 0 us
  starting transfers between devices: 0.04 us -> 22.4 us
  Pallas kernels: 0 us -> 18.9 us
  local copies, waits for them, and re-layouts: 0.01 us -> 15.9 us
  between operations: 13.5 us -> 0.15 us
    all_gather x2 -> x0, waiting for transfers between devices: 90.4 us -> none  [the longest x1 62.3 us: on_device(): panel_full = lax.all_gather(panel_cols, 'col', axis=1, tiled=True)]
    ppermute x0 -> x40, waiting for transfers between devices: none -> 35.8 us  [send(): return lax.ppermute(value, axis, pairs)]
    dot_general x7 -> x0, matrix products: 27.9 us -> none  [product(): return jnp.dot(left, right, preferred_element_type=jnp.float32)]
    ppermute x0 -> x40, starting transfers between devices: none -> 22.4 us  [send(): return lax.ppermute(value, axis, pairs)]
    pallas_call x0 -> x7, Pallas kernels: none -> 18.9 us  [the longest x6 16.5 us: update(): pl.pallas_call(functools.partial(update_kernel, len(pieces)), grid=(rows...]
    unnamed x4 -> x24, local copies, waits for them, and re-layouts: 0.01 us -> 13.8 us
    slice x0 -> x2, local copies, waits for them, and re-layouts: none -> 2.11 us  [on_device(): held = [source[:, start:start + size] for start, size in group]]
    unnamed x2 -> x0, waiting for transfers between devices: 1.41 us -> none
  transfers between devices with their start and end apart: 2 -> 40, of which waited for: 2 -> 15; matrix products, arithmetic and copies ran while one was open for 5% -> 1% of each run, Pallas kernels for 0% -> 17%
where the time goes in v1:
time: 94.2 us; the launch traced here: 93.2 us
  waiting for transfers between devices  35.8 us (38%)
  starting transfers between devices  22.4 us (24%)
  Pallas kernels  18.9 us (20%)
  local copies, waits for them, and re-layouts  15.9 us (17%)
    ppermute x40, waiting for transfers between devices, send(): return lax.ppermute(value, axis, pairs)  35.8 us
    ppermute x40, starting transfers between devices, send(): return lax.ppermute(value, axis, pairs)  22.4 us
    pallas_call x6, Pallas kernels, update(): pl.pallas_call(functools.partial(update_kernel, len(pieces)), grid=(rows...  16.5 us
    unnamed x24, local copies, waits for them, and re-layouts  13.8 us
    pallas_call x1, Pallas kernels, weights(): pl.pallas_call(functools.partial(weights_kernel, len(heads), chips), out_...  2.37 us
    slice x2, local copies, waits for them, and re-layouts, on_device(): held = [source[:, start:start + size] for start, size in group]  2.11 us
  transfers between devices with their start and end apart: 40, of which 15 were waited for; matrix products, arithmetic and copies ran while one was open for 1% of the time, Pallas kernels for 17%

profile of v1, /device:TPU:0, one launch (start us, length us, event | category | flops | bytes accessed | tf_op | source)
XLA Modules:
  0.0 93.2 jit_solution(9985933384020364344)
XLA Ops:
  0.0 1.1 %fusion = (bf16[64,1024]{1,0:T(8,128)(2,1)S(1)}, bf16[64,1024]{1,0:T(8,128)(2,1)S(1)}, bf16[64,1024]{1,0:T(8,128)(2,1)S(1)}) fusion(bf16[64,6144]{1,0:T(8,128)(2,1)} %bitcast.3), kind=kLoop, calls=%fused_computation.1 | loop fusion | bytes 786432 | tf_op jit(solution)/shard_map/slice | solution.py:127
  1.1 3.1 %collective-permute-start = (bf16[64,1024]{1,0:T(8,128)(2,1)S(1)}, bf16[64,1024]{1,0:T(8,128)(2,1)S(1)}, u32[]{:S(2)}, u32[]{:S(2)}) collective-permute-start(bf16[64,1024]{1,0:T(8,128)(2,1)S(1)} %get-tuple-element.13), channel_id=1, source_target_pairs={{0,2},{1,3},{2,4},{3,5},{4,6},{5,7},{6,0},{7,1},{8,10},{9,11},{10,... | collective-permute-start | bytes 393224 | tf_op jit(solution)/shard_map/ppermute | solution.py:120
  4.2 1.6 %collective-permute-start.29 = (bf16[64,1024]{1,0:T(8,128)(2,1)S(1)}, bf16[64,1024]{1,0:T(8,128)(2,1)S(1)}, u32[]{:S(2)}, u32[]{:S(2)}) collective-permute-start(bf16[64,1024]{1,0:T(8,128)(2,1)S(1)} %get-tuple-element.11), channel_id=1, source_target_pairs={{0,2},{1,3},{2,4},{3,5},{4,6},{5,7},{6,0},{7,1},{8,10},{9,11},{10,... | collective-permute-start | bytes 393224 | tf_op jit(solution)/shard_map/ppermute | solution.py:120
  5.7 1.6 %collective-permute-start.5 = (bf16[64,1024]{1,0:T(8,128)(2,1)S(1)}, bf16[64,1024]{1,0:T(8,128)(2,1)S(1)}, u32[]{:S(2)}, u32[]{:S(2)}) collective-permute-start(bf16[64,1024]{1,0:T(8,128)(2,1)S(1)} %get-tuple-element.12), channel_id=1, source_target_pairs={{0,2},{1,3},{2,4},{3,5},{4,6},{5,7},{6,0},{7,1},{8,10},{9,11},{10,... | collective-permute-start | bytes 393224 | tf_op jit(solution)/shard_map/ppermute | solution.py:120
  7.3 3.2 %collective-permute-done.refs_2_ = bf16[64,1024]{1,0:T(8,128)(2,1)S(1)} collective-permute-done((bf16[64,1024]{1,0:T(8,128)(2,1)S(1)}, bf16[64,1024]{1,0:T(8,128)(2,1)S(1)}, u32[]{:S(2)}, u32[]{:S(2)}) %collective-permute-start) | collective-permute-done | bytes 131104 | tf_op jit(solution)/shard_map/ppermute | solution.py:120
  10.5 2.8 %collective-permute-done.29.refs_2_ = bf16[64,1024]{1,0:T(8,128)(2,1)S(1)} collective-permute-done((bf16[64,1024]{1,0:T(8,128)(2,1)S(1)}, bf16[64,1024]{1,0:T(8,128)(2,1)S(1)}, u32[]{:S(2)}, u32[]{:S(2)}) %collective-permute-start.29) | collective-permute-done | bytes 131104 | tf_op jit(solution)/shard_map/ppermute | solution.py:120
  13.4 2.8 %collective-permute-done.5.refs_2_ = bf16[64,1024]{1,0:T(8,128)(2,1)S(1)} collective-permute-done((bf16[64,1024]{1,0:T(8,128)(2,1)S(1)}, bf16[64,1024]{1,0:T(8,128)(2,1)S(1)}, u32[]{:S(2)}, u32[]{:S(2)}) %collective-permute-start.5) | collective-permute-done | bytes 131104 | tf_op jit(solution)/shard_map/ppermute | solution.py:120
  16.2 1.7 %collective-permute-start.1 = (bf16[128,1024]{1,0:T(8,128)(2,1)}, bf16[128,1024]{1,0:T(8,128)(2,1)S(1)}, u32[]{:S(2)}, u32[]{:S(2)}) collective-permute-start(bf16[128,1024]{1,0:T(8,128)(2,1)} %refs_0_), channel_id=1, source_target_pairs={{0,8},{8,0},{16,24},{24,16},{1,9},{9,1},{17,25},{25,17},{2,10},{10... | collective-permute-start | bytes 786440 | tf_op jit(solution)/shard_map/ppermute | solution.py:120
  17.9 1.1 %collective-permute-done.36.refs_4_ = bf16[64,1024]{1,0:T(8,128)(2,1)S(1)} collective-permute-done((bf16[64,1024]{1,0:T(8,128)(2,1)S(1)}, bf16[64,1024]{1,0:T(8,128)(2,1)S(1)}, u32[]{:S(2)}, u32[]{:S(2)}) %collective-permute-start.36) | collective-permute-done | bytes 131104 | tf_op jit(solution)/shard_map/ppermute | solution.py:120
  19.0 1.7 %collective-permute-start.2 = (bf16[128,1024]{1,0:T(8,128)(2,1)}, bf16[128,1024]{1,0:T(8,128)(2,1)S(1)}, u32[]{:S(2)}, u32[]{:S(2)}) collective-permute-start(bf16[128,1024]{1,0:T(8,128)(2,1)} %refs_0_), channel_id=1, source_target_pairs={{0,16},{8,24},{16,0},{24,8},{1,17},{9,25},{17,1},{25,9},{2,18},{10... | collective-permute-start | bytes 786440 | tf_op jit(solution)/shard_map/ppermute | solution.py:120
  20.9 2.4 %collective-permute-start.3 = (bf16[128,1024]{1,0:T(8,128)(2,1)}, bf16[128,1024]{1,0:T(8,128)(2,1)S(1)}, u32[]{:S(2)}, u32[]{:S(2)}) collective-permute-start(bf16[128,1024]{1,0:T(8,128)(2,1)} %refs_0_), channel_id=1, source_target_pairs={{0,24},{8,16},{16,8},{24,0},{1,25},{9,17},{17,9},{25,1},{2,26},{10... | collective-permute-start | bytes 786440 | tf_op jit(solution)/shard_map/ppermute | solution.py:120
  23.4 2.4 %collective-permute-done.6.refs_4_ = bf16[64,1024]{1,0:T(8,128)(2,1)S(1)} collective-permute-done((bf16[64,1024]{1,0:T(8,128)(2,1)S(1)}, bf16[64,1024]{1,0:T(8,128)(2,1)S(1)}, u32[]{:S(2)}, u32[]{:S(2)}) %collective-permute-start.6) | collective-permute-done | bytes 131104 | tf_op jit(solution)/shard_map/ppermute | solution.py:120
  25.8 0.6 collective-permute-start.37
  26.3 5.1 %collective-permute-done.2.refs_2_ = bf16[128,1024]{1,0:T(8,128)(2,1)S(1)} collective-permute-done((bf16[128,1024]{1,0:T(8,128)(2,1)}, bf16[128,1024]{1,0:T(8,128)(2,1)S(1)}, u32[]{:S(2)}, u32[]{:S(2)}) %collective-permute-start.2) | collective-permute-done | bytes 262176 | tf_op jit(solution)/shard_map/ppermute | solution.py:120
  31.4 0.7 copy-done.8
  32.1 0.8 collective-permute-start.33
  33.0 0.7 copy-done.10
  33.9 1.5 %collective-permute-start.27 = (bf16[64,1024]{1,0:T(8,128)(2,1)S(1)}, bf16[64,1024]{1,0:T(8,128)(2,1)S(1)}, u32[]{:S(2)}, u32[]{:S(2)}) collective-permute-start(bf16[64,1024]{1,0:T(8,128)(2,1)S(1)} %collective-permute-done.6.refs_4_), channel_id=1, source_target_pairs={{0,2},{1,3},{2,4},{3,5},{4,6},{5,7},{6,0},{7,1},{8,10},{9,11},{10,... | collective-permute-start | bytes 393224 | tf_op jit(solution)/shard_map/ppermute | solution.py:120
  35.7 1.1 %fusion.1 = (bf16[64,1024]{1,0:T(8,128)(2,1)S(1)}, bf16[64,1024]{1,0:T(8,128)(2,1)S(1)}, bf16[64,1024]{1,0:T(8,128)(2,1)S(1)}) fusion(bf16[64,6144]{1,0:T(8,128)(2,1)} %bitcast.5), kind=kLoop, calls=%fused_computation.2 | loop fusion | bytes 786432 | tf_op jit(solution)/shard_map/slice | solution.py:127
  36.7 2.5 %collective-permute-done.33.refs_6_ = bf16[64,1024]{1,0:T(8,128)(2,1)S(1)} collective-permute-done((bf16[64,1024]{1,0:T(8,128)(2,1)S(1)}, bf16[64,1024]{1,0:T(8,128)(2,1)S(1)}, u32[]{:S(2)}, u32[]{:S(2)}) %collective-permute-start.33) | collective-permute-done | bytes 131104 | tf_op jit(solution)/shard_map/ppermute | solution.py:120
  39.2 0.9 collective-permute-start.13
  40.2 1.8 %collective-permute-done.27.refs_6_ = bf16[64,1024]{1,0:T(8,128)(2,1)S(1)} collective-permute-done((bf16[64,1024]{1,0:T(8,128)(2,1)S(1)}, bf16[64,1024]{1,0:T(8,128)(2,1)S(1)}, u32[]{:S(2)}, u32[]{:S(2)}) %collective-permute-start.27) | collective-permute-done | bytes 131104 | tf_op jit(solution)/shard_map/ppermute | solution.py:120
  41.9 0.7 collective-permute-start.7
  42.7 3.6 %collective-permute-done.19.refs_2_ = bf16[64,1024]{1,0:T(8,128)(2,1)S(1)} collective-permute-done((bf16[64,1024]{1,0:T(8,128)(2,1)S(1)}, bf16[64,1024]{1,0:T(8,128)(2,1)S(1)}, u32[]{:S(2)}, u32[]{:S(2)}) %collective-permute-start.19) | collective-permute-done | bytes 131104 | tf_op jit(solution)/shard_map/ppermute | solution.py:120
  46.3 2.6 %collective-permute-done.13.refs_2_ = bf16[64,1024]{1,0:T(8,128)(2,1)S(1)} collective-permute-done((bf16[64,1024]{1,0:T(8,128)(2,1)S(1)}, bf16[64,1024]{1,0:T(8,128)(2,1)S(1)}, u32[]{:S(2)}, u32[]{:S(2)}) %collective-permute-start.13) | collective-permute-done | bytes 131104 | tf_op jit(solution)/shard_map/ppermute | solution.py:120
  48.9 1.4 %collective-permute-done.7.refs_2_ = bf16[64,1024]{1,0:T(8,128)(2,1)S(1)} collective-permute-done((bf16[64,1024]{1,0:T(8,128)(2,1)S(1)}, bf16[64,1024]{1,0:T(8,128)(2,1)S(1)}, u32[]{:S(2)}, u32[]{:S(2)}) %collective-permute-start.7) | collective-permute-done | bytes 131104 | tf_op jit(solution)/shard_map/ppermute | solution.py:120
  50.3 1.6 %collective-permute-start.15 = (bf16[64,1024]{1,0:T(8,128)(2,1)S(1)}, bf16[64,1024]{1,0:T(8,128)(2,1)S(1)}, u32[]{:S(2)}, u32[]{:S(2)}) collective-permute-start(bf16[64,1024]{1,0:T(8,128)(2,1)S(1)} %collective-permute-done.13.refs_2_), channel_id=1, source_target_pairs={{0,2},{1,3},{2,4},{3,5},{4,6},{5,7},{6,0},{7,1},{8,10},{9,11},{10,... | collective-permute-start | bytes 393224 | tf_op jit(solution)/shard_map/ppermute | solution.py:120
  51.9 1.2 %collective-permute-start.9 = (bf16[64,1024]{1,0:T(8,128)(2,1)S(1)}, bf16[64,1024]{1,0:T(8,128)(2,1)S(1)}, u32[]{:S(2)}, u32[]{:S(2)}) collective-permute-start(bf16[64,1024]{1,0:T(8,128)(2,1)S(1)} %collective-permute-done.7.refs_2_), channel_id=1, source_target_pairs={{0,2},{1,3},{2,4},{3,5},{4,6},{5,7},{6,0},{7,1},{8,10},{9,11},{10,... | collective-permute-start | bytes 393224 | tf_op jit(solution)/shard_map/ppermute | solution.py:120
  53.2 5.3 %collective-permute-done.21.refs_4_ = bf16[64,1024]{1,0:T(8,128)(2,1)S(1)} collective-permute-done((bf16[64,1024]{1,0:T(8,128)(2,1)S(1)}, bf16[64,1024]{1,0:T(8,128)(2,1)S(1)}, u32[]{:S(2)}, u32[]{:S(2)}) %collective-permute-start.21) | collective-permute-done | bytes 131104 | tf_op jit(solution)/shard_map/ppermute | solution.py:120
  58.5 0.9 %copy-done.2 = bf16[128,1024]{1,0:T(8,128)(2,1)S(1)} copy-done((bf16[128,1024]{1,0:T(8,128)(2,1)S(1)}, bf16[128,1024]{1,0:T(8,128)(2,1)}, u32[]{:S(2)}) %copy-start.2) | copy-done | bytes 262168
  59.4 0.9 %copy-done.3 = bf16[2,256,256]{2,1,0:T(8,128)(2,1)S(1)} copy-done((bf16[2,256,256]{2,1,0:T(8,128)(2,1)S(1)}, bf16[2,256,256]{2,1,0:T(8,128)(2,1)}, u32[]{:S(2)}) %copy-start.3) | copy-done | bytes 262168
  60.4 0.9 %copy-done.4 = bf16[2,256,256]{2,1,0:T(8,128)(2,1)S(1)} copy-done((bf16[2,256,256]{2,1,0:T(8,128)(2,1)S(1)}, bf16[2,256,256]{2,1,0:T(8,128)(2,1)}, u32[]{:S(2)}) %copy-start.4) | copy-done | bytes 262168
  61.3 0.9 %copy-done.5 = bf16[2,256,256]{2,1,0:T(8,128)(2,1)S(1)} copy-done((bf16[2,256,256]{2,1,0:T(8,128)(2,1)S(1)}, bf16[2,256,256]{2,1,0:T(8,128)(2,1)}, u32[]{:S(2)}) %copy-start.5) | copy-done | bytes 262168
  62.3 0.9 %copy-done.7 = bf16[128,1024]{1,0:T(8,128)(2,1)S(1)} copy-done((bf16[128,1024]{1,0:T(8,128)(2,1)S(1)}, bf16[128,1024]{1,0:T(8,128)(2,1)}, u32[]{:S(2)}) %copy-start.7) | copy-done | bytes 262168
  63.2 0.9 %copy-done.9 = bf16[128,1024]{1,0:T(8,128)(2,1)S(1)} copy-done((bf16[128,1024]{1,0:T(8,128)(2,1)S(1)}, bf16[128,1024]{1,0:T(8,128)(2,1)}, u32[]{:S(2)}) %copy-start.9) | copy-done | bytes 262168
  64.2 0.9 %copy-done.11 = bf16[128,1024]{1,0:T(8,128)(2,1)S(1)} copy-done((bf16[128,1024]{1,0:T(8,128)(2,1)S(1)}, bf16[128,1024]{1,0:T(8,128)(2,1)}, u32[]{:S(2)}) %copy-start.11) | copy-done | bytes 262168
  65.1 2.4 %weights.1.weights_ref = bf16[512,1024]{1,0:T(8,128)(2,1)S(1)} custom-call(s32[2]{0:T(128)S(1)} %pad_add_fusion.ids_ref, bf16[128,1024]{1,0:T(8,128)(2,1)S(1)} %copy-done.2, bf16[128,1024]{1,0:T(8,128)(2,1)S(1)} %copy-done.7, bf16[128,1024]{1,0:T(8,128)(2,1)S(1)} %copy-done.9, bf16[128,1024]{1,0:T(8,128)(2,1)S(1)} %copy-done.11, ...), custom_call_target="tpu_custom_call" | custom-call | flops 1342177280 | bytes 2097152 | tf_op jit(solution)/shard_map/weights/pallas_call | solution.py:56
  67.7 4.6 %copy-done = bf16[6144,1024]{1,0:T(8,128)(2,1)S(1)} copy-done((bf16[6144,1024]{1,0:T(8,128)(2,1)S(1)}, bf16[6144,1024]{1,0:T(8,128)(2,1)}, u32[]{:S(2)}) %copy-start) | copy-done | bytes 12582936
  72.2 1.1 %copy-done.1 = bf16[6144,64]{0,1:T(8,128)(2,1)S(1)} copy-done((bf16[6144,64]{0,1:T(8,128)(2,1)S(1)}, bf16[6144,64]{0,1:T(8,128)(2,1)}, u32[]{:S(2)}) %copy-start.1) | copy-done | bytes 786456
  73.4 3.4 %update.6.refs_8_ = bf16[6144,1024]{1,0:T(8,128)(2,1)} custom-call(bf16[6144,1024]{1,0:T(8,128)(2,1)S(1)} %copy-done, bf16[512,1024]{1,0:T(8,128)(2,1)S(1)} %weights.1.weights_ref, bf16[64,6144]{1,0:T(8,128)(2,1)S(1)} %bitcast.6, bf16[64,6144]{1,0:T(8,128)(2,1)S(1)} %collective-permute-done.4.refs_1_, bf16[64,1024]{1,0:T(8,128)(2,1)S(1)} %collective-permute-done.refs_2_, ...), custom_call_target="tpu_custom_call" | custom-call | flops 1073741824 | bytes 4194304 | tf_op jit(solution)/shard_map/update/pallas_call | solution.py:92
  77.2 0.5 collective-permute-start.11
  77.8 2.6 %update.7.refs_8_ = bf16[6144,1024]{1,0:T(8,128)(2,1)} custom-call(bf16[6144,1024]{1,0:T(8,128)(2,1)S(1)} %copy-done, bf16[512,1024]{1,0:T(8,128)(2,1)S(1)} %weights.1.weights_ref, bf16[64,6144]{1,0:T(8,128)(2,1)S(1)} %bitcast.7, bf16[64,6144]{1,0:T(8,128)(2,1)S(1)} %collective-permute-done.4.refs_1_, ...), custom_call_target="tpu_custom_call", output_to_operand_aliasing={{}: (10, {})} | custom-call | flops 1073741824 | bytes 4194304 | tf_op jit(solution)/shard_map/update/pallas_call | solution.py:92
  80.9 2.6 %update.8.refs_8_ = bf16[6144,1024]{1,0:T(8,128)(2,1)} custom-call(bf16[6144,1024]{1,0:T(8,128)(2,1)S(1)} %copy-done, bf16[512,1024]{1,0:T(8,128)(2,1)S(1)} %weights.1.weights_ref, bf16[64,6144]{1,0:T(8,128)(2,1)S(1)} %bitcast.8, bf16[64,6144]{1,0:T(8,128)(2,1)S(1)} %collective-permute-done.4.refs_1_, ...), custom_call_target="tpu_custom_call", output_to_operand_aliasing={{}: (10, {})} | custom-call | flops 1073741824 | bytes 4194304 | tf_op jit(solution)/shard_map/update/pallas_call | solution.py:92
  84.0 0.7 collective-permute-done.11.refs_6_
  84.7 0.5 collective-permute-start.12
  85.2 2.6 %update.9.refs_8_ = bf16[6144,1024]{1,0:T(8,128)(2,1)} custom-call(bf16[6144,1024]{1,0:T(8,128)(2,1)S(1)} %copy-done, bf16[512,1024]{1,0:T(8,128)(2,1)S(1)} %weights.1.weights_ref, bf16[64,6144]{1,0:T(8,128)(2,1)S(1)} %bitcast.9, bf16[64,6144]{1,0:T(8,128)(2,1)S(1)} %collective-permute-done.4.refs_1_, ...), custom_call_target="tpu_custom_call", output_to_operand_aliasing={{}: (10, {})} | custom-call | flops 1073741824 | bytes 4194304 | tf_op jit(solution)/shard_map/update/pallas_call | solution.py:92
  87.9 2.6 %update.10.refs_8_ = bf16[6144,1024]{1,0:T(8,128)(2,1)} custom-call(bf16[6144,1024]{1,0:T(8,128)(2,1)S(1)} %copy-done, bf16[512,1024]{1,0:T(8,128)(2,1)S(1)} %weights.1.weights_ref, bf16[64,6144]{1,0:T(8,128)(2,1)S(1)} %bitcast.10, bf16[64,6144]{1,0:T(8,128)(2,1)S(1)} %collective-permute-done.4.refs_1_, ...), custom_call_target="tpu_custom_call", output_to_operand_aliasing={{}: (10, {})} | custom-call | flops 1073741824 | bytes 4194304 | tf_op jit(solution)/shard_map/update/pallas_call | solution.py:92
  90.5 2.7 %update.11 = bf16[6144,1024]{1,0:T(8,128)(2,1)} custom-call(bf16[6144,1024]{1,0:T(8,128)(2,1)S(1)} %copy-done, bf16[512,1024]{1,0:T(8,128)(2,1)S(1)} %weights.1.weights_ref, bf16[64,6144]{1,0:T(8,128)(2,1)S(1)} %bitcast.11, bf16[64,6144]{1,0:T(8,128)(2,1)S(1)} %collective-permute-done.4.refs_1_, ...), custom_call_target="tpu_custom_call", output_to_operand_aliasing={{}: (10, {})} | custom-call | flops 1073741824 | bytes 4194304 | tf_op jit(solution)/shard_map/update/pallas_call | solution.py:92
  (66 shorter events, 2.5 us)
Async XLA Ops:
  1.1 9.5 %collective-permute-start = (bf16[64,1024]{1,0:T(8,128)(2,1)S(1)}, bf16[64,1024]{1,0:T(8,128)(2,1)S(1)}, u32[]{:S(2)}, u32[]{:S(2)}) collective-permute-start(bf16[64,1024]{1,0:T(8,128)(2,1)S(1)} %get-tuple-element.13), channel_id=1, source_target_pairs={{0,2},{1,3},{2,4},{3,5},{4,6},{5,7},{6,0},{7,1},{8,10},{9,11},{10,... | collective-permute-start | bytes 393224 | tf_op jit(solution)/shard_map/ppermute | solution.py:120
  4.2 9.2 %collective-permute-start.29 = (bf16[64,1024]{1,0:T(8,128)(2,1)S(1)}, bf16[64,1024]{1,0:T(8,128)(2,1)S(1)}, u32[]{:S(2)}, u32[]{:S(2)}) collective-permute-start(bf16[64,1024]{1,0:T(8,128)(2,1)S(1)} %get-tuple-element.11), channel_id=1, source_target_pairs={{0,2},{1,3},{2,4},{3,5},{4,6},{5,7},{6,0},{7,1},{8,10},{9,11},{10,... | collective-permute-start | bytes 393224 | tf_op jit(solution)/shard_map/ppermute | solution.py:120
  5.7 10.4 %collective-permute-start.5 = (bf16[64,1024]{1,0:T(8,128)(2,1)S(1)}, bf16[64,1024]{1,0:T(8,128)(2,1)S(1)}, u32[]{:S(2)}, u32[]{:S(2)}) collective-permute-start(bf16[64,1024]{1,0:T(8,128)(2,1)S(1)} %get-tuple-element.12), channel_id=1, source_target_pairs={{0,2},{1,3},{2,4},{3,5},{4,6},{5,7},{6,0},{7,1},{8,10},{9,11},{10,... | collective-permute-start | bytes 393224 | tf_op jit(solution)/shard_map/ppermute | solution.py:120
  10.5 8.4 %collective-permute-start.36 = (bf16[64,1024]{1,0:T(8,128)(2,1)S(1)}, bf16[64,1024]{1,0:T(8,128)(2,1)S(1)}, u32[]{:S(2)}, u32[]{:S(2)}) collective-permute-start(bf16[64,1024]{1,0:T(8,128)(2,1)S(1)} %collective-permute-done.refs_2_), channel_id=1, source_target_pairs={{0,2},{1,3},{2,4},{3,5},{4,6},{5,7},{6,0},{7,1},{8,10},{9,11},{10,... | collective-permute-start | bytes 393224 | tf_op jit(solution)/shard_map/ppermute | solution.py:120
  10.5 8.4 %collective-permute-start.35 = (bf16[64,1024]{1,0:T(8,128)(2,1)S(1)}, bf16[64,1024]{1,0:T(8,128)(2,1)S(1)}, u32[]{:S(2)}, u32[]{:S(2)}) collective-permute-start(bf16[64,1024]{1,0:T(8,128)(2,1)S(1)} %collective-permute-done.refs_2_), channel_id=1, source_target_pairs={{0,1},{1,0},{2,3},{3,2},{4,5},{5,4},{6,7},{7,6},{8,9},{9,8},{10,11... | collective-permute-start | bytes 393224 | tf_op jit(solution)/shard_map/ppermute | solution.py:120
  13.3 7.6 %collective-permute-start.31 = (bf16[64,1024]{1,0:T(8,128)(2,1)S(1)}, bf16[64,1024]{1,0:T(8,128)(2,1)S(1)}, u32[]{:S(2)}, u32[]{:S(2)}) collective-permute-start(bf16[64,1024]{1,0:T(8,128)(2,1)S(1)} %collective-permute-done.29.refs_2_), channel_id=1, source_target_pairs={{0,2},{1,3},{2,4},{3,5},{4,6},{5,7},{6,0},{7,1},{8,10},{9,11},{10,... | collective-permute-start | bytes 393224 | tf_op jit(solution)/shard_map/ppermute | solution.py:120
  13.4 10.0 %collective-permute-start.30 = (bf16[64,1024]{1,0:T(8,128)(2,1)S(1)}, bf16[64,1024]{1,0:T(8,128)(2,1)S(1)}, u32[]{:S(2)}, u32[]{:S(2)}) collective-permute-start(bf16[64,1024]{1,0:T(8,128)(2,1)S(1)} %collective-permute-done.29.refs_2_), channel_id=1, source_target_pairs={{0,1},{1,0},{2,3},{3,2},{4,5},{5,4},{6,7},{7,6},{8,9},{9,8},{10,11... | collective-permute-start | bytes 393224 | tf_op jit(solution)/shard_map/ppermute | solution.py:120
  16.2 9.6 %collective-permute-start.1 = (bf16[128,1024]{1,0:T(8,128)(2,1)}, bf16[128,1024]{1,0:T(8,128)(2,1)S(1)}, u32[]{:S(2)}, u32[]{:S(2)}) collective-permute-start(bf16[128,1024]{1,0:T(8,128)(2,1)} %refs_0_), channel_id=1, source_target_pairs={{0,8},{8,0},{16,24},{24,16},{1,9},{9,1},{17,25},{25,17},{2,10},{10... | collective-permute-start | bytes 786440 | tf_op jit(solution)/shard_map/ppermute | solution.py:120
  19.0 6.8 %collective-permute-start.6 = (bf16[64,1024]{1,0:T(8,128)(2,1)S(1)}, bf16[64,1024]{1,0:T(8,128)(2,1)S(1)}, u32[]{:S(2)}, u32[]{:S(2)}) collective-permute-start(bf16[64,1024]{1,0:T(8,128)(2,1)S(1)} %collective-permute-done.5.refs_2_), channel_id=1, source_target_pairs={{0,2},{1,3},{2,4},{3,5},{4,6},{5,7},{6,0},{7,1},{8,10},{9,11},{10,... | collective-permute-start | bytes 393224 | tf_op jit(solution)/shard_map/ppermute | solution.py:120
  19.0 12.5 %collective-permute-start.2 = (bf16[128,1024]{1,0:T(8,128)(2,1)}, bf16[128,1024]{1,0:T(8,128)(2,1)S(1)}, u32[]{:S(2)}, u32[]{:S(2)}) collective-permute-start(bf16[128,1024]{1,0:T(8,128)(2,1)} %refs_0_), channel_id=1, source_target_pairs={{0,16},{8,24},{16,0},{24,8},{1,17},{9,25},{17,1},{25,9},{2,18},{10... | collective-permute-start | bytes 786440 | tf_op jit(solution)/shard_map/ppermute | solution.py:120
  20.9 12.0 %collective-permute-start.3 = (bf16[128,1024]{1,0:T(8,128)(2,1)}, bf16[128,1024]{1,0:T(8,128)(2,1)S(1)}, u32[]{:S(2)}, u32[]{:S(2)}) collective-permute-start(bf16[128,1024]{1,0:T(8,128)(2,1)} %refs_0_), channel_id=1, source_target_pairs={{0,24},{8,16},{16,8},{24,0},{1,25},{9,17},{17,9},{25,1},{2,26},{10... | collective-permute-start | bytes 786440 | tf_op jit(solution)/shard_map/ppermute | solution.py:120
  23.4 2.4 %collective-permute-start.25 = (bf16[64,1024]{1,0:T(8,128)(2,1)S(1)}, bf16[64,1024]{1,0:T(8,128)(2,1)S(1)}, u32[]{:S(2)}, u32[]{:S(2)}) collective-permute-start(bf16[64,1024]{1,0:T(8,128)(2,1)S(1)} %collective-permute-done.5.refs_2_), channel_id=1, source_target_pairs={{0,1},{1,0},{2,3},{3,2},{4,5},{5,4},{6,7},{7,6},{8,9},{9,8},{10,11... | collective-permute-start | bytes 393224 | tf_op jit(solution)/shard_map/ppermute | solution.py:120
  25.7 41.8 %collective-permute-start.4 = (bf16[64,6144]{1,0:T(8,128)(2,1)}, bf16[64,6144]{1,0:T(8,128)(2,1)S(1)}, u32[]{:S(2)}, u32[]{:S(2)}) collective-permute-start(bf16[64,6144]{1,0:T(8,128)(2,1)} %bitcast.4), channel_id=1, source_target_pairs={{0,1},{1,0},{2,3},{3,2},{4,5},{5,4},{6,7},{7,6},{8,9},{9,8},{10,11... | collective-permute-start | bytes 2359304 | tf_op jit(solution)/shard_map/ppermute | solution.py:120
  25.7 8.2 %collective-permute-start.38 = (bf16[64,1024]{1,0:T(8,128)(2,1)S(1)}, bf16[64,1024]{1,0:T(8,128)(2,1)S(1)}, u32[]{:S(2)}, u32[]{:S(2)}) collective-permute-start(bf16[64,1024]{1,0:T(8,128)(2,1)S(1)} %collective-permute-done.36.refs_4_), channel_id=1, source_target_pairs={{0,2},{1,3},{2,4},{3,5},{4,6},{5,7},{6,0},{7,1},{8,10},{9,11},{10,... | collective-permute-start | bytes 393224 | tf_op jit(solution)/shard_map/ppermute | solution.py:120
  25.8 13.5 %copy-start.6 = (bf16[128,1024]{1,0:T(8,128)(2,1)}, bf16[128,1024]{1,0:T(8,128)(2,1)S(1)}, u32[]{:S(2)}) copy-start(bf16[128,1024]{1,0:T(8,128)(2,1)S(1)} %collective-permute-done.1.refs_1_) | copy-start | bytes 786436
  25.8 9.7 %collective-permute-start.37 = (bf16[64,1024]{1,0:T(8,128)(2,1)S(1)}, bf16[64,1024]{1,0:T(8,128)(2,1)S(1)}, u32[]{:S(2)}, u32[]{:S(2)}) collective-permute-start(bf16[64,1024]{1,0:T(8,128)(2,1)S(1)} %collective-permute-done.36.refs_4_), channel_id=1, source_target_pairs={{0,1},{1,0},{2,3},{3,2},{4,5},{5,4},{6,7},{7,6},{8,9},{9,8},{10,11... | collective-permute-start | bytes 393224 | tf_op jit(solution)/shard_map/ppermute | solution.py:120
  32.1 7.1 %collective-permute-start.33 = (bf16[64,1024]{1,0:T(8,128)(2,1)S(1)}, bf16[64,1024]{1,0:T(8,128)(2,1)S(1)}, u32[]{:S(2)}, u32[]{:S(2)}) collective-permute-start(bf16[64,1024]{1,0:T(8,128)(2,1)S(1)} %collective-permute-done.31.refs_4_), channel_id=1, source_target_pairs={{0,2},{1,3},{2,4},{3,5},{4,6},{5,7},{6,0},{7,1},{8,10},{9,11},{10,... | collective-permute-start | bytes 393224 | tf_op jit(solution)/shard_map/ppermute | solution.py:120
  33.6 5.6 %collective-permute-start.32 = (bf16[64,1024]{1,0:T(8,128)(2,1)S(1)}, bf16[64,1024]{1,0:T(8,128)(2,1)S(1)}, u32[]{:S(2)}, u32[]{:S(2)}) collective-permute-start(bf16[64,1024]{1,0:T(8,128)(2,1)S(1)} %collective-permute-done.31.refs_4_), channel_id=1, source_target_pairs={{0,1},{1,0},{2,3},{3,2},{4,5},{5,4},{6,7},{7,6},{8,9},{9,8},{10,11... | collective-permute-start | bytes 393224 | tf_op jit(solution)/shard_map/ppermute | solution.py:120
  33.9 8.0 %collective-permute-start.27 = (bf16[64,1024]{1,0:T(8,128)(2,1)S(1)}, bf16[64,1024]{1,0:T(8,128)(2,1)S(1)}, u32[]{:S(2)}, u32[]{:S(2)}) collective-permute-start(bf16[64,1024]{1,0:T(8,128)(2,1)S(1)} %collective-permute-done.6.refs_4_), channel_id=1, source_target_pairs={{0,2},{1,3},{2,4},{3,5},{4,6},{5,7},{6,0},{7,1},{8,10},{9,11},{10,... | collective-permute-start | bytes 393224 | tf_op jit(solution)/shard_map/ppermute | solution.py:120
  35.4 7.2 %collective-permute-start.26 = (bf16[64,1024]{1,0:T(8,128)(2,1)S(1)}, bf16[64,1024]{1,0:T(8,128)(2,1)S(1)}, u32[]{:S(2)}, u32[]{:S(2)}) collective-permute-start(bf16[64,1024]{1,0:T(8,128)(2,1)S(1)} %collective-permute-done.6.refs_4_), channel_id=1, source_target_pairs={{0,1},{1,0},{2,3},{3,2},{4,5},{5,4},{6,7},{7,6},{8,9},{9,8},{10,11... | collective-permute-start | bytes 393224 | tf_op jit(solution)/shard_map/ppermute | solution.py:120
  39.2 7.1 %collective-permute-start.19 = (bf16[64,1024]{1,0:T(8,128)(2,1)S(1)}, bf16[64,1024]{1,0:T(8,128)(2,1)S(1)}, u32[]{:S(2)}, u32[]{:S(2)}) collective-permute-start(bf16[64,1024]{1,0:T(8,128)(2,1)S(1)} %get-tuple-element.14), channel_id=1, source_target_pairs={{0,2},{1,3},{2,4},{3,5},{4,6},{5,7},{6,0},{7,1},{8,10},{9,11},{10,... | collective-permute-start | bytes 393224 | tf_op jit(solution)/shard_map/ppermute | solution.py:120
  39.2 9.6 %collective-permute-start.13 = (bf16[64,1024]{1,0:T(8,128)(2,1)S(1)}, bf16[64,1024]{1,0:T(8,128)(2,1)S(1)}, u32[]{:S(2)}, u32[]{:S(2)}) collective-permute-start(bf16[64,1024]{1,0:T(8,128)(2,1)S(1)} %get-tuple-element.15), channel_id=1, source_target_pairs={{0,2},{1,3},{2,4},{3,5},{4,6},{5,7},{6,0},{7,1},{8,10},{9,11},{10,... | collective-permute-start | bytes 393224 | tf_op jit(solution)/shard_map/ppermute | solution.py:120
  41.9 8.3 %collective-permute-start.7 = (bf16[64,1024]{1,0:T(8,128)(2,1)S(1)}, bf16[64,1024]{1,0:T(8,128)(2,1)S(1)}, u32[]{:S(2)}, u32[]{:S(2)}) collective-permute-start(bf16[64,1024]{1,0:T(8,128)(2,1)S(1)} %get-tuple-element.16), channel_id=1, source_target_pairs={{0,2},{1,3},{2,4},{3,5},{4,6},{5,7},{6,0},{7,1},{8,10},{9,11},{10,... | collective-permute-start | bytes 393224 | tf_op jit(solution)/shard_map/ppermute | solution.py:120
  42.7 7.6 %collective-permute-start.39 = (bf16[64,1024]{1,0:T(8,128)(2,1)S(1)}, bf16[64,1024]{1,0:T(8,128)(2,1)}, u32[]{:S(2)}, u32[]{:S(2)}) collective-permute-start(bf16[64,1024]{1,0:T(8,128)(2,1)S(1)} %collective-permute-done.38.refs_6_), channel_id=1, source_target_pairs={{0,1},{1,0},{2,3},{3,2},{4,5},{5,4},{6,7},{7,6},{8,9},{9,8},{10,11... | collective-permute-start | bytes 393224 | tf_op jit(solution)/shard_map/ppermute | solution.py:120
  46.3 5.6 %collective-permute-start.34 = (bf16[64,1024]{1,0:T(8,128)(2,1)S(1)}, bf16[64,1024]{1,0:T(8,128)(2,1)S(1)}, u32[]{:S(2)}, u32[]{:S(2)}) collective-permute-start(bf16[64,1024]{1,0:T(8,128)(2,1)S(1)} %collective-permute-done.33.refs_6_), channel_id=1, source_target_pairs={{0,1},{1,0},{2,3},{3,2},{4,5},{5,4},{6,7},{7,6},{8,9},{9,8},{10,11... | collective-permute-start | bytes 393224 | tf_op jit(solution)/shard_map/ppermute | solution.py:120
  48.9 3.1 %collective-permute-start.28 = (bf16[64,1024]{1,0:T(8,128)(2,1)S(1)}, bf16[64,1024]{1,0:T(8,128)(2,1)S(1)}, u32[]{:S(2)}, u32[]{:S(2)}) collective-permute-start(bf16[64,1024]{1,0:T(8,128)(2,1)S(1)} %collective-permute-done.27.refs_6_), channel_id=1, source_target_pairs={{0,1},{1,0},{2,3},{3,2},{4,5},{5,4},{6,7},{7,6},{8,9},{9,8},{10,11... | collective-permute-start | bytes 393224 | tf_op jit(solution)/shard_map/ppermute | solution.py:120
  50.3 8.2 %collective-permute-start.21 = (bf16[64,1024]{1,0:T(8,128)(2,1)S(1)}, bf16[64,1024]{1,0:T(8,128)(2,1)S(1)}, u32[]{:S(2)}, u32[]{:S(2)}) collective-permute-start(bf16[64,1024]{1,0:T(8,128)(2,1)S(1)} %collective-permute-done.19.refs_2_), channel_id=1, source_target_pairs={{0,2},{1,3},{2,4},{3,5},{4,6},{5,7},{6,0},{7,1},{8,10},{9,11},{10,... | collective-permute-start | bytes 393224 | tf_op jit(solution)/shard_map/ppermute | solution.py:120
  50.3 17.2 %collective-permute-start.15 = (bf16[64,1024]{1,0:T(8,128)(2,1)S(1)}, bf16[64,1024]{1,0:T(8,128)(2,1)S(1)}, u32[]{:S(2)}, u32[]{:S(2)}) collective-permute-start(bf16[64,1024]{1,0:T(8,128)(2,1)S(1)} %collective-permute-done.13.refs_2_), channel_id=1, source_target_pairs={{0,2},{1,3},{2,4},{3,5},{4,6},{5,7},{6,0},{7,1},{8,10},{9,11},{10,... | collective-permute-start | bytes 393224 | tf_op jit(solution)/shard_map/ppermute | solution.py:120
  51.9 24.8 %collective-permute-start.20 = (bf16[64,1024]{1,0:T(8,128)(2,1)S(1)}, bf16[64,1024]{1,0:T(8,128)(2,1)S(1)}, u32[]{:S(2)}, u32[]{:S(2)}) collective-permute-start(bf16[64,1024]{1,0:T(8,128)(2,1)S(1)} %collective-permute-done.19.refs_2_), channel_id=1, source_target_pairs={{0,1},{1,0},{2,3},{3,2},{4,5},{5,4},{6,7},{7,6},{8,9},{9,8},{10,11... | collective-permute-start | bytes 393224 | tf_op jit(solution)/shard_map/ppermute | solution.py:120
  51.9 25.2 %collective-permute-start.9 = (bf16[64,1024]{1,0:T(8,128)(2,1)S(1)}, bf16[64,1024]{1,0:T(8,128)(2,1)S(1)}, u32[]{:S(2)}, u32[]{:S(2)}) collective-permute-start(bf16[64,1024]{1,0:T(8,128)(2,1)S(1)} %collective-permute-done.7.refs_2_), channel_id=1, source_target_pairs={{0,2},{1,3},{2,4},{3,5},{4,6},{5,7},{6,0},{7,1},{8,10},{9,11},{10,... | collective-permute-start | bytes 393224 | tf_op jit(solution)/shard_map/ppermute | solution.py:120
  58.4 19.3 %collective-permute-start.23 = (bf16[64,1024]{1,0:T(8,128)(2,1)S(1)}, bf16[64,1024]{1,0:T(8,128)(2,1)S(1)}, u32[]{:S(2)}, u32[]{:S(2)}) collective-permute-start(bf16[64,1024]{1,0:T(8,128)(2,1)S(1)} %collective-permute-done.21.refs_4_), channel_id=1, source_target_pairs={{0,2},{1,3},{2,4},{3,5},{4,6},{5,7},{6,0},{7,1},{8,10},{9,11},{10,... | collective-permute-start | bytes 393224 | tf_op jit(solution)/shard_map/ppermute | solution.py:120
  58.5 1.0 %copy-start.2 = (bf16[128,1024]{1,0:T(8,128)(2,1)S(1)}, bf16[128,1024]{1,0:T(8,128)(2,1)}, u32[]{:S(2)}) copy-start(bf16[128,1024]{1,0:T(8,128)(2,1)} %refs_0_) | copy-start | bytes 786436
  59.4 0.9 %copy-start.3 = (bf16[2,256,256]{2,1,0:T(8,128)(2,1)S(1)}, bf16[2,256,256]{2,1,0:T(8,128)(2,1)}, u32[]{:S(2)}) copy-start(bf16[2,256,256]{2,1,0:T(8,128)(2,1)} %refs_4_.1) | copy-start | bytes 786436
  60.4 0.9 %copy-start.4 = (bf16[2,256,256]{2,1,0:T(8,128)(2,1)S(1)}, bf16[2,256,256]{2,1,0:T(8,128)(2,1)}, u32[]{:S(2)}) copy-start(bf16[2,256,256]{2,1,0:T(8,128)(2,1)} %refs_5_.1) | copy-start | bytes 786436
  61.3 0.9 %copy-start.5 = (bf16[2,256,256]{2,1,0:T(8,128)(2,1)S(1)}, bf16[2,256,256]{2,1,0:T(8,128)(2,1)}, u32[]{:S(2)}) copy-start(bf16[2,256,256]{2,1,0:T(8,128)(2,1)} %refs_6_.1) | copy-start | bytes 786436
  62.3 0.9 %copy-start.7 = (bf16[128,1024]{1,0:T(8,128)(2,1)S(1)}, bf16[128,1024]{1,0:T(8,128)(2,1)}, u32[]{:S(2)}) copy-start(bf16[128,1024]{1,0:T(8,128)(2,1)} %copy-done.6) | copy-start | bytes 786436
  67.5 12.9 %collective-permute-start.14 = (bf16[64,1024]{1,0:T(8,128)(2,1)S(1)}, bf16[64,1024]{1,0:T(8,128)(2,1)S(1)}, u32[]{:S(2)}, u32[]{:S(2)}) collective-permute-start(bf16[64,1024]{1,0:T(8,128)(2,1)S(1)} %collective-permute-done.13.refs_2_), channel_id=1, source_target_pairs={{0,1},{1,0},{2,3},{3,2},{4,5},{5,4},{6,7},{7,6},{8,9},{9,8},{10,11... | collective-permute-start | bytes 393224 | tf_op jit(solution)/shard_map/ppermute | solution.py:120
  67.6 13.3 %collective-permute-start.17 = (bf16[64,1024]{1,0:T(8,128)(2,1)S(1)}, bf16[64,1024]{1,0:T(8,128)(2,1)S(1)}, u32[]{:S(2)}, u32[]{:S(2)}) collective-permute-start(bf16[64,1024]{1,0:T(8,128)(2,1)S(1)} %collective-permute-done.15.refs_4_), channel_id=1, source_target_pairs={{0,2},{1,3},{2,4},{3,5},{4,6},{5,7},{6,0},{7,1},{8,10},{9,11},{10,... | collective-permute-start | bytes 393224 | tf_op jit(solution)/shard_map/ppermute | solution.py:120
  67.6 4.6 %copy-start = (bf16[6144,1024]{1,0:T(8,128)(2,1)S(1)}, bf16[6144,1024]{1,0:T(8,128)(2,1)}, u32[]{:S(2)}) copy-start(bf16[6144,1024]{1,0:T(8,128)(2,1)} %slab_ref.11) | copy-start | bytes 37748740
  72.2 1.1 %copy-start.1 = (bf16[6144,64]{0,1:T(8,128)(2,1)S(1)}, bf16[6144,64]{0,1:T(8,128)(2,1)}, u32[]{:S(2)}) copy-start(bf16[6144,64]{0,1:T(8,128)(2,1)} %param.7) | copy-start | bytes 2359300
  76.7 6.8 %collective-permute-start.22 = (bf16[64,1024]{1,0:T(8,128)(2,1)S(1)}, bf16[64,1024]{1,0:T(8,128)(2,1)S(1)}, u32[]{:S(2)}, u32[]{:S(2)}) collective-permute-start(bf16[64,1024]{1,0:T(8,128)(2,1)S(1)} %collective-permute-done.21.refs_4_), channel_id=1, source_target_pairs={{0,1},{1,0},{2,3},{3,2},{4,5},{5,4},{6,7},{7,6},{8,9},{9,8},{10,11... | collective-permute-start | bytes 393224 | tf_op jit(solution)/shard_map/ppermute | solution.py:120
  77.2 7.6 %collective-permute-start.11 = (bf16[64,1024]{1,0:T(8,128)(2,1)S(1)}, bf16[64,1024]{1,0:T(8,128)(2,1)S(1)}, u32[]{:S(2)}, u32[]{:S(2)}) collective-permute-start(bf16[64,1024]{1,0:T(8,128)(2,1)S(1)} %collective-permute-done.9.refs_4_), channel_id=1, source_target_pairs={{0,2},{1,3},{2,4},{3,5},{4,6},{5,7},{6,0},{7,1},{8,10},{9,11},{10,... | collective-permute-start | bytes 393224 | tf_op jit(solution)/shard_map/ppermute | solution.py:120
  77.7 7.0 %collective-permute-start.24 = (bf16[64,1024]{1,0:T(8,128)(2,1)S(1)}, bf16[64,1024]{1,0:T(8,128)(2,1)S(1)}, u32[]{:S(2)}, u32[]{:S(2)}) collective-permute-start(bf16[64,1024]{1,0:T(8,128)(2,1)S(1)} %collective-permute-done.23.refs_6_), channel_id=1, source_target_pairs={{0,1},{1,0},{2,3},{3,2},{4,5},{5,4},{6,7},{7,6},{8,9},{9,8},{10,11... | collective-permute-start | bytes 393224 | tf_op jit(solution)/shard_map/ppermute | solution.py:120
  80.4 7.5 %collective-permute-start.16 = (bf16[64,1024]{1,0:T(8,128)(2,1)S(1)}, bf16[64,1024]{1,0:T(8,128)(2,1)S(1)}, u32[]{:S(2)}, u32[]{:S(2)}) collective-permute-start(bf16[64,1024]{1,0:T(8,128)(2,1)S(1)} %collective-permute-done.15.refs_4_), channel_id=1, source_target_pairs={{0,1},{1,0},{2,3},{3,2},{4,5},{5,4},{6,7},{7,6},{8,9},{9,8},{10,11... | collective-permute-start | bytes 393224 | tf_op jit(solution)/shard_map/ppermute | solution.py:120
  80.8 7.0 %collective-permute-start.18 = (bf16[64,1024]{1,0:T(8,128)(2,1)S(1)}, bf16[64,1024]{1,0:T(8,128)(2,1)S(1)}, u32[]{:S(2)}, u32[]{:S(2)}) collective-permute-start(bf16[64,1024]{1,0:T(8,128)(2,1)S(1)} %collective-permute-done.17.refs_6_), channel_id=1, source_target_pairs={{0,1},{1,0},{2,3},{3,2},{4,5},{5,4},{6,7},{7,6},{8,9},{9,8},{10,11... | collective-permute-start | bytes 393224 | tf_op jit(solution)/shard_map/ppermute | solution.py:120
  83.5 7.0 %collective-permute-start.8 = (bf16[64,1024]{1,0:T(8,128)(2,1)S(1)}, bf16[64,1024]{1,0:T(8,128)(2,1)S(1)}, u32[]{:S(2)}, u32[]{:S(2)}) collective-permute-start(bf16[64,1024]{1,0:T(8,128)(2,1)S(1)} %collective-permute-done.7.refs_2_), channel_id=1, source_target_pairs={{0,1},{1,0},{2,3},{3,2},{4,5},{5,4},{6,7},{7,6},{8,9},{9,8},{10,11... | collective-permute-start | bytes 393224 | tf_op jit(solution)/shard_map/ppermute | solution.py:120
  84.7 5.8 %collective-permute-start.10 = (bf16[64,1024]{1,0:T(8,128)(2,1)S(1)}, bf16[64,1024]{1,0:T(8,128)(2,1)S(1)}, u32[]{:S(2)}, u32[]{:S(2)}) collective-permute-start(bf16[64,1024]{1,0:T(8,128)(2,1)S(1)} %collective-permute-done.9.refs_4_), channel_id=1, source_target_pairs={{0,1},{1,0},{2,3},{3,2},{4,5},{5,4},{6,7},{7,6},{8,9},{9,8},{10,11... | collective-permute-start | bytes 393224 | tf_op jit(solution)/shard_map/ppermute | solution.py:120
  84.7 5.8 %collective-permute-start.12 = (bf16[64,1024]{1,0:T(8,128)(2,1)S(1)}, bf16[64,1024]{1,0:T(8,128)(2,1)S(1)}, u32[]{:S(2)}, u32[]{:S(2)}) collective-permute-start(bf16[64,1024]{1,0:T(8,128)(2,1)S(1)} %collective-permute-done.11.refs_6_), channel_id=1, source_target_pairs={{0,1},{1,0},{2,3},{3,2},{4,5},{5,4},{6,7},{7,6},{8,9},{9,8},{10,11... | collective-permute-start | bytes 393224 | tf_op jit(solution)/shard_map/ppermute | solution.py:120
  (4 other events, 3.3 us)
